TPU v7x, 32 devices: a whole 2x2x4 slice. The times are simulated.
32 devices in a mesh: segment: 2 (over x), slab: 16 (over z, y, core).
Axes of the slice: x: 2, y: 2, z: 4, core: 2. Of those that a mesh axis runs over, the one named last changes fastest.
Arguments:
- activations: bfloat16 [2, 2, 64, 8, 8, 128], P('segment', None, 'slab'), may hold values from -6 to 6
- weights: bfloat16 [2, 3456, 128], P('segment'), may hold values from -0.109375 to 0.109375
- out_grad: bfloat16 [2, 64, 8, 8, 128], P(None, 'slab'), may hold values from -6 to 6
Outputs:
- update: float32 [2, 3456, 128], P('segment')
- input_grads: bfloat16 [2, 2, 64, 8, 8, 128], P('segment', None, 'slab')
All inputs are finite; a program needn't handle non-finite values.
Results may differ from a plain program's by a relative error of at most 0.017.
Values may be sent and summed in bfloat16 or wider, within the bound.
No kernel may reach another device: no remote copies, remote signals or barrier semaphores. Data moves between devices by JAX's collectives and lax.ppermute only.
A program may use at most 64 MiB of HBM per device.

v0:
```python
import math
import jax
import jax.numpy as jnp
from jax import lax
from jax.sharding import PartitionSpec as P


def padded(cells, sides, width):
    for axis, dim in sides:
        count = lax.axis_size(axis)
        ends = count - 1
        head = lax.slice_in_dim(cells, 0, width, axis=dim)
        tail = lax.slice_in_dim(cells, cells.shape[dim] - width, cells.shape[dim], axis=dim)
        cells = jnp.concatenate(
            [
                lax.ppermute(tail, axis, [(i, (i + 1) % count) for i in range(ends)]),
                cells,
                lax.ppermute(head, axis, [((i + 1) % count, i) for i in range(ends)]),
            ],
            axis=dim,
        )
    return cells


def from_behind(block, axis, distance):
    devices = range(lax.axis_size(axis))
    route = [(i - distance, i) for i in devices if i - distance in devices]
    return lax.ppermute(block, axis, route)


def patches_of(rimmed):
    depth_count = rimmed.shape[0] - 2
    width_count = rimmed.shape[1]
    height = rimmed.shape[2]
    padded_all = jnp.pad(rimmed, ((0, 0), (1, 1), (1, 1), (0, 0)))
    pieces = []
    for offset in range(27):
        depth_off = offset // 9
        width_off = offset // 3 % 3
        height_off = offset % 3
        pieces.append(
            padded_all[
                depth_off : depth_off + depth_count,
                width_off : width_off + width_count,
                height_off : height_off + height,
            ]
        )
    joined = jnp.concatenate(pieces, axis=-1)
    return joined.reshape(depth_count * width_count * height, joined.shape[-1])


def shards(activations, weights, out_grad):
    stored_inputs = activations[0]
    weight = weights[0]
    channels = weight.shape[1]
    micro_count, depth_count, width_count, height = stored_inputs.shape[:4]
    cell_count = depth_count * width_count * height
    segments = lax.axis_size("segment")
    sindex = lax.axis_index("segment")
    flipped = (
        weight.reshape(27, channels, channels)[::-1]
        .transpose(0, 2, 1)
        .reshape(27 * channels, channels)
    )

    def advance(counter, state_tuple):
        incoming, partial_value, gradients = state_tuple
        micro_index = counter - (segments - 1 - sindex)
        active = (micro_index >= 0) & (micro_index < micro_count)
        chosen = jnp.clip(micro_index, 0, micro_count - 1)
        one_input = lax.dynamic_index_in_dim(stored_inputs, chosen, 0, False)
        rimmed_one = padded(one_input, (("slab", 0),), 1)
        patches = patches_of(rimmed_one)
        preact = jnp.dot(patches, weight, preferred_element_type=jnp.float32)
        from_loss = lax.dynamic_index_in_dim(out_grad, chosen, 0, False)
        upstream = (
            jnp.where(sindex == segments - 1, from_loss, incoming)
            .astype(jnp.float32)
            .reshape(cell_count, channels)
        )
        sigval = jax.nn.sigmoid(preact)
        deltas = jnp.where(active, upstream * sigval * (1.0 + preact * (1.0 - sigval)), 0.0).astype(
            jnp.bfloat16
        )
        partial_value = partial_value + lax.dot_general(
            patches, deltas, (((0,), (0,)), ((), ())), preferred_element_type=jnp.float32
        )
        delta_rim = padded(
            deltas.reshape(depth_count, width_count, height, channels), (("slab", 0),), 1
        )
        backward = jnp.dot(patches_of(delta_rim), flipped, preferred_element_type=jnp.float32)
        result = (
            (upstream + backward)
            .astype(jnp.bfloat16)
            .reshape(depth_count, width_count, height, channels)
        )
        current = lax.dynamic_index_in_dim(gradients, chosen, 0, False)
        gradients = lax.dynamic_update_index_in_dim(
            gradients, jnp.where(active, result, current), chosen, 0
        )
        incoming = from_behind(result, "segment", -1)
        return (incoming, partial_value, gradients)

    start_state = (
        jnp.zeros((depth_count, width_count, height, channels), jnp.bfloat16),
        jnp.zeros((27 * channels, channels), jnp.float32),
        jnp.zeros(stored_inputs.shape, jnp.bfloat16),
    )
    final_state = lax.fori_loop(0, segments + micro_count - 1, advance, start_state)
    partial_value = final_state[1]
    gradients = final_state[2]
    bound_value = math.sqrt(27.0 * channels * channels * segments)
    summed = lax.psum(partial_value, "slab")
    squares = lax.psum(jnp.sum(summed * summed), "segment")
    factor = jnp.minimum(1.0, bound_value / (jnp.sqrt(squares) + 1e-06))
    update = summed * factor
    return (update[None], gradients[None])


def solution(mesh):
    return jax.shard_map(
        shards,
        mesh=mesh,
        in_specs=(
            P("segment", None, "slab", None, None, None),
            P("segment", None, None),
            P(None, "slab", None, None, None),
        ),
        out_specs=(P("segment", None, None), P("segment", None, "slab", None, None, None)),
        check_vma=False,
    )
```

profile of v0, /device:TPU:0, one launch (start us, length us, event | category | flops | bytes accessed | tf_op | source)
XLA Modules:
  0.0 205.5 jit_solution(9570711436723103198)
XLA Ops:
  7.2 0.0 all-reduce.4.cloned.1.call-start
  7.2 2.3 %copy.5 = bf16[27,128,128]{1,2,0:T(8,128)(2,1)} copy(bf16[27,128,128]{2,1,0:T(8,128)(2,1)} %bitcast.282) | data formatting | bytes 1769472 | tf_op jit(solution)/shard_map/reshape;squeeze | solution.py:61
  9.5 1.2 rev.3
  10.8 71.9 %while.20 = (s32[]{:T(128)}, bf16[4,8,8,128]{3,2,1,0:T(8,128)(2,1)S(1)}, f32[3456,128]{1,0:T(8,128)S(1)}, bf16[2,4,8,8,128]{4,3,2,1,0:T(8,128)(2,1)S(1)}, pred[]...) while((s32[]{:T(128)}, ...), condition=%wide.region_1.2_spmd.clone, body=%wide.region_0.1_spmd.clone.sunk | while | flops 684656640 | bytes 30519764 | solution.py:109
  10.9 1.3 collective-permute-start
  12.2 3.0 %collective-permute-start.1 = (bf16[1,8,8,128]{3,2,1,0:T(8,128)(2,1)S(1)}, bf16[1,8,8,128]{3,2,1,0:T(8,128)(2,1)S(1)}, u32[]{:S(2)}, u32[]{:S(2)}) collective-permute-start(bf16[1,8,8,128]{3,2,1,0:T(8,128)(2,1)S(1)} %get-tuple-element.463), channel_id=1, source_target_pairs={{0,1},{1,2},{2,3},{3,4},{4,5},{5,6},{6,7},{7,8},{8,9},{9,10},{10,1... | collective-permute-start | bytes 49160 | tf_op jit(solution)/shard_map/while/body/eval_jaxpr/ppermute | solution.py:16
  15.3 0.7 collective-permute-done.1
  16.0 0.1 fusion.54
  16.1 0.1 fusion.55
  16.2 0.2 fusion.56
  17.1 0.5 copy-done.4
  17.6 0.7 fusion.57
  18.3 1.3 collective-permute-start.2
  19.6 5.1 %collective-permute-start.3 = (bf16[1,8,8,128]{3,2,1,0:T(8,128)(2,1)S(1)}, bf16[1,8,8,128]{3,2,1,0:T(8,128)(2,1)S(1)}, u32[]{:S(2)}, u32[]{:S(2)}) collective-permute-start(bf16[1,8,8,128]{3,2,1,0:T(8,128)(2,1)S(1)} %get-tuple-element.492), channel_id=1, source_target_pairs={{0,1},{1,2},{2,3},{3,4},{4,5},{5,6},{6,7},{7,8},{8,9},{9,10},{10,1... | collective-permute-start | bytes 49160 | tf_op jit(solution)/shard_map/while/body/eval_jaxpr/ppermute | solution.py:16
  24.8 1.2 convolution_add_fusion.3
  26.0 0.1 select_maximum_fusion.3
  26.1 0.1 fusion.58
  26.1 0.2 fusion.59
  26.7 0.1 fusion.60
  27.1 0.6 fusion.61
  27.7 1.3 collective-permute-start.4
  29.1 4.8 %collective-permute-done.4 = bf16[4,8,8,128]{3,2,1,0:T(8,128)(2,1)S(1)} collective-permute-done((bf16[4,8,8,128]{3,2,1,0:T(8,128)(2,1)S(1)}, bf16[4,8,8,128]{3,2,1,0:T(8,128)(2,1)S(1)}, u32[]{:S(2)}, u32[]{:S(2)}) %collective-permute-start.4) | collective-permute-done | bytes 65568 | tf_op jit(solution)/shard_map/while/body/eval_jaxpr/ppermute | solution.py:28
  33.9 1.3 collective-permute-start
  35.2 3.7 %collective-permute-start.1 = (bf16[1,8,8,128]{3,2,1,0:T(8,128)(2,1)S(1)}, bf16[1,8,8,128]{3,2,1,0:T(8,128)(2,1)S(1)}, u32[]{:S(2)}, u32[]{:S(2)}) collective-permute-start(bf16[1,8,8,128]{3,2,1,0:T(8,128)(2,1)S(1)} %get-tuple-element.463), channel_id=1, source_target_pairs={{0,1},{1,2},{2,3},{3,4},{4,5},{5,6},{6,7},{7,8},{8,9},{9,10},{10,1... | collective-permute-start | bytes 49160 | tf_op jit(solution)/shard_map/while/body/eval_jaxpr/ppermute | solution.py:16
  39.0 0.7 collective-permute-done.1
  39.7 0.1 fusion.54
  39.8 0.1 fusion.55
  39.9 0.2 fusion.56
  40.8 0.5 copy-done.4
  41.3 0.7 fusion.57
  42.0 1.3 collective-permute-start.2
  43.3 6.1 %collective-permute-start.3 = (bf16[1,8,8,128]{3,2,1,0:T(8,128)(2,1)S(1)}, bf16[1,8,8,128]{3,2,1,0:T(8,128)(2,1)S(1)}, u32[]{:S(2)}, u32[]{:S(2)}) collective-permute-start(bf16[1,8,8,128]{3,2,1,0:T(8,128)(2,1)S(1)} %get-tuple-element.492), channel_id=1, source_target_pairs={{0,1},{1,2},{2,3},{3,4},{4,5},{5,6},{6,7},{7,8},{8,9},{9,10},{10,1... | collective-permute-start | bytes 49160 | tf_op jit(solution)/shard_map/while/body/eval_jaxpr/ppermute | solution.py:16
  49.4 1.2 convolution_add_fusion.3
  50.6 0.1 select_maximum_fusion.3
  50.7 0.1 fusion.58
  50.7 0.2 fusion.59
  51.3 0.1 fusion.60
  51.7 0.6 fusion.61
  52.3 1.3 collective-permute-start.4
  53.7 4.8 %collective-permute-done.4 = bf16[4,8,8,128]{3,2,1,0:T(8,128)(2,1)S(1)} collective-permute-done((bf16[4,8,8,128]{3,2,1,0:T(8,128)(2,1)S(1)}, bf16[4,8,8,128]{3,2,1,0:T(8,128)(2,1)S(1)}, u32[]{:S(2)}, u32[]{:S(2)}) %collective-permute-start.4) | collective-permute-done | bytes 65568 | tf_op jit(solution)/shard_map/while/body/eval_jaxpr/ppermute | solution.py:28
  58.5 1.3 collective-permute-start
  59.8 3.7 %collective-permute-start.1 = (bf16[1,8,8,128]{3,2,1,0:T(8,128)(2,1)S(1)}, bf16[1,8,8,128]{3,2,1,0:T(8,128)(2,1)S(1)}, u32[]{:S(2)}, u32[]{:S(2)}) collective-permute-start(bf16[1,8,8,128]{3,2,1,0:T(8,128)(2,1)S(1)} %get-tuple-element.463), channel_id=1, source_target_pairs={{0,1},{1,2},{2,3},{3,4},{4,5},{5,6},{6,7},{7,8},{8,9},{9,10},{10,1... | collective-permute-start | bytes 49160 | tf_op jit(solution)/shard_map/while/body/eval_jaxpr/ppermute | solution.py:16
  63.6 0.7 collective-permute-done.1
  64.3 0.1 fusion.54
  64.4 0.1 fusion.55
  64.5 0.2 fusion.56
  65.4 0.5 copy-done.4
  65.9 0.7 fusion.57
  66.6 1.3 collective-permute-start.2
  67.9 5.7 %collective-permute-start.3 = (bf16[1,8,8,128]{3,2,1,0:T(8,128)(2,1)S(1)}, bf16[1,8,8,128]{3,2,1,0:T(8,128)(2,1)S(1)}, u32[]{:S(2)}, u32[]{:S(2)}) collective-permute-start(bf16[1,8,8,128]{3,2,1,0:T(8,128)(2,1)S(1)} %get-tuple-element.492), channel_id=1, source_target_pairs={{0,1},{1,2},{2,3},{3,4},{4,5},{5,6},{6,7},{7,8},{8,9},{9,10},{10,1... | collective-permute-start | bytes 49160 | tf_op jit(solution)/shard_map/while/body/eval_jaxpr/ppermute | solution.py:16
  73.6 1.2 convolution_add_fusion.3
  74.8 0.1 select_maximum_fusion.3
  74.9 0.1 fusion.58
  74.9 0.2 fusion.59
  75.5 0.1 fusion.60
  75.9 0.6 fusion.61
  76.5 1.3 collective-permute-start.4
  77.9 4.8 %collective-permute-done.4 = bf16[4,8,8,128]{3,2,1,0:T(8,128)(2,1)S(1)} collective-permute-done((bf16[4,8,8,128]{3,2,1,0:T(8,128)(2,1)S(1)}, bf16[4,8,8,128]{3,2,1,0:T(8,128)(2,1)S(1)}, u32[]{:S(2)}, u32[]{:S(2)}) %collective-permute-start.4) | collective-permute-done | bytes 65568 | tf_op jit(solution)/shard_map/while/body/eval_jaxpr/ppermute | solution.py:28
  82.7 1.2 copy-done
  83.9 0.0 all-reduce.4.cloned.1.call-update
  83.9 104.4 %all-reduce.4.cloned.1.call-done = f32[3456,128]{1,0:T(8,128)} async-done(((f32[3456,128]{1,0:T(8,128)}), f32[3456,128]{1,0:T(8,128)}) %all-reduce.4.cloned.1.call-update) | async-done | bytes 1769488 | tf_op jit(solution)/shard_map/psum | solution.py:113
  188.3 2.7 %multiply_reduce_fusion = f32[]{:T(128)} fusion(f32[3456,128]{1,0:T(8,128)} %all-reduce.4.cloned.1.call-done), kind=kLoop, calls=%fused_computation.95 | loop fusion | flops 884735 | bytes 1769476 | tf_op jit(solution)/shard_map/reduce_sum | solution.py:114
  191.0 5.6 %psum.15 = f32[]{:T(128)} all-reduce(f32[]{:T(128)} %multiply_reduce_fusion), channel_id=1, replica_groups=mesh['segment'=2,'slab'=16] {'segment'}, use_global_device_ids=true, to_apply=%region_4.5 | all-reduce | flops 1 | bytes 8 | tf_op jit(solution)/shard_map/psum | solution.py:114
  197.3 1.3 multiply_bitcast_fusion
  (207 shorter events, 3.5 us)
Async XLA Ops:
  7.2 181.2 %all-reduce.4.cloned.1.call-start = ((), (), s32[]{:S(2)}) async-start(), calls=%async_computation | async-start | bytes 3538944 | tf_op jit(solution)/shard_map/psum | solution.py:113
  7.2 3.6 %copy-start.2 = (bf16[1,2,4,8,8,128]{5,4,3,2,1,0:T(8,128)(2,1)S(1)}, bf16[1,2,4,8,8,128]{5,4,3,2,1,0:T(8,128)(2,1)}, u32[]{:S(2)}) copy-start(bf16[1,2,4,8,8,128]{5,4,3,2,1,0:T(8,128)(2,1)} %param.5) | copy-start | bytes 393220
  7.2 3.6 %copy-start.5 = (bf16[2,4,8,8,128]{4,3,2,1,0:T(8,128)(2,1)S(1)}, bf16[2,4,8,8,128]{4,3,2,1,0:T(8,128)(2,1)}, u32[]{:S(2)}) copy-start(bf16[2,4,8,8,128]{4,3,2,1,0:T(8,128)(2,1)} %param.7) | copy-start | bytes 393220
  10.9 4.4 %collective-permute-start = (bf16[1,8,8,128]{3,2,1,0:T(8,128)(2,1)S(1)}, bf16[1,8,8,128]{3,2,1,0:T(8,128)(2,1)S(1)}, u32[]{:S(2)}, u32[]{:S(2)}) collective-permute-start(bf16[1,8,8,128]{3,2,1,0:T(8,128)(2,1)S(1)} %get-tuple-element.462), channel_id=1, source_target_pairs={{1,0},{2,1},{3,2},{4,3},{5,4},{6,5},{7,6},{8,7},{9,8},{10,9},{11,1... | collective-permute-start | bytes 49160 | tf_op jit(solution)/shard_map/while/body/eval_jaxpr/ppermute | solution.py:18
  12.2 3.9 %collective-permute-start.1 = (bf16[1,8,8,128]{3,2,1,0:T(8,128)(2,1)S(1)}, bf16[1,8,8,128]{3,2,1,0:T(8,128)(2,1)S(1)}, u32[]{:S(2)}, u32[]{:S(2)}) collective-permute-start(bf16[1,8,8,128]{3,2,1,0:T(8,128)(2,1)S(1)} %get-tuple-element.463), channel_id=1, source_target_pairs={{0,1},{1,2},{2,3},{3,4},{4,5},{5,6},{6,7},{7,8},{8,9},{9,10},{10,1... | collective-permute-start | bytes 49160 | tf_op jit(solution)/shard_map/while/body/eval_jaxpr/ppermute | solution.py:16
  16.4 1.2 copy-start.4
  18.3 7.6 %collective-permute-start.2 = (bf16[1,8,8,128]{3,2,1,0:T(8,128)(2,1)S(1)}, bf16[1,8,8,128]{3,2,1,0:T(8,128)(2,1)S(1)}, u32[]{:S(2)}, u32[]{:S(2)}) collective-permute-start(bf16[1,8,8,128]{3,2,1,0:T(8,128)(2,1)S(1)} %get-tuple-element.491), channel_id=1, source_target_pairs={{1,0},{2,1},{3,2},{4,3},{5,4},{6,5},{7,6},{8,7},{9,8},{10,9},{11,1... | collective-permute-start | bytes 49160 | tf_op jit(solution)/shard_map/while/body/eval_jaxpr/ppermute | solution.py:18
  19.6 6.3 %collective-permute-start.3 = (bf16[1,8,8,128]{3,2,1,0:T(8,128)(2,1)S(1)}, bf16[1,8,8,128]{3,2,1,0:T(8,128)(2,1)S(1)}, u32[]{:S(2)}, u32[]{:S(2)}) collective-permute-start(bf16[1,8,8,128]{3,2,1,0:T(8,128)(2,1)S(1)} %get-tuple-element.492), channel_id=1, source_target_pairs={{0,1},{1,2},{2,3},{3,4},{4,5},{5,6},{6,7},{7,8},{8,9},{9,10},{10,1... | collective-permute-start | bytes 49160 | tf_op jit(solution)/shard_map/while/body/eval_jaxpr/ppermute | solution.py:16
  27.7 6.2 %collective-permute-start.4 = (bf16[4,8,8,128]{3,2,1,0:T(8,128)(2,1)S(1)}, bf16[4,8,8,128]{3,2,1,0:T(8,128)(2,1)S(1)}, u32[]{:S(2)}, u32[]{:S(2)}) collective-permute-start(bf16[4,8,8,128]{3,2,1,0:T(8,128)(2,1)S(1)} %bitcast.225), channel_id=1, source_target_pairs={{16,0},{17,1},{18,2},{19,3},{20,4},{21,5},{22,6},{23,7},{24,8},{25... | collective-permute-start | bytes 196616 | tf_op jit(solution)/shard_map/while/body/eval_jaxpr/ppermute | solution.py:28
  33.9 5.1 %collective-permute-start = (bf16[1,8,8,128]{3,2,1,0:T(8,128)(2,1)S(1)}, bf16[1,8,8,128]{3,2,1,0:T(8,128)(2,1)S(1)}, u32[]{:S(2)}, u32[]{:S(2)}) collective-permute-start(bf16[1,8,8,128]{3,2,1,0:T(8,128)(2,1)S(1)} %get-tuple-element.462), channel_id=1, source_target_pairs={{1,0},{2,1},{3,2},{4,3},{5,4},{6,5},{7,6},{8,7},{9,8},{10,9},{11,1... | collective-permute-start | bytes 49160 | tf_op jit(solution)/shard_map/while/body/eval_jaxpr/ppermute | solution.py:18
  35.2 4.5 %collective-permute-start.1 = (bf16[1,8,8,128]{3,2,1,0:T(8,128)(2,1)S(1)}, bf16[1,8,8,128]{3,2,1,0:T(8,128)(2,1)S(1)}, u32[]{:S(2)}, u32[]{:S(2)}) collective-permute-start(bf16[1,8,8,128]{3,2,1,0:T(8,128)(2,1)S(1)} %get-tuple-element.463), channel_id=1, source_target_pairs={{0,1},{1,2},{2,3},{3,4},{4,5},{5,6},{6,7},{7,8},{8,9},{9,10},{10,1... | collective-permute-start | bytes 49160 | tf_op jit(solution)/shard_map/while/body/eval_jaxpr/ppermute | solution.py:16
  40.1 1.2 copy-start.4
  42.0 8.6 %collective-permute-start.2 = (bf16[1,8,8,128]{3,2,1,0:T(8,128)(2,1)S(1)}, bf16[1,8,8,128]{3,2,1,0:T(8,128)(2,1)S(1)}, u32[]{:S(2)}, u32[]{:S(2)}) collective-permute-start(bf16[1,8,8,128]{3,2,1,0:T(8,128)(2,1)S(1)} %get-tuple-element.491), channel_id=1, source_target_pairs={{1,0},{2,1},{3,2},{4,3},{5,4},{6,5},{7,6},{8,7},{9,8},{10,9},{11,1... | collective-permute-start | bytes 49160 | tf_op jit(solution)/shard_map/while/body/eval_jaxpr/ppermute | solution.py:18
  43.3 7.3 %collective-permute-start.3 = (bf16[1,8,8,128]{3,2,1,0:T(8,128)(2,1)S(1)}, bf16[1,8,8,128]{3,2,1,0:T(8,128)(2,1)S(1)}, u32[]{:S(2)}, u32[]{:S(2)}) collective-permute-start(bf16[1,8,8,128]{3,2,1,0:T(8,128)(2,1)S(1)} %get-tuple-element.492), channel_id=1, source_target_pairs={{0,1},{1,2},{2,3},{3,4},{4,5},{5,6},{6,7},{7,8},{8,9},{9,10},{10,1... | collective-permute-start | bytes 49160 | tf_op jit(solution)/shard_map/while/body/eval_jaxpr/ppermute | solution.py:16
  52.3 6.2 %collective-permute-start.4 = (bf16[4,8,8,128]{3,2,1,0:T(8,128)(2,1)S(1)}, bf16[4,8,8,128]{3,2,1,0:T(8,128)(2,1)S(1)}, u32[]{:S(2)}, u32[]{:S(2)}) collective-permute-start(bf16[4,8,8,128]{3,2,1,0:T(8,128)(2,1)S(1)} %bitcast.225), channel_id=1, source_target_pairs={{16,0},{17,1},{18,2},{19,3},{20,4},{21,5},{22,6},{23,7},{24,8},{25... | collective-permute-start | bytes 196616 | tf_op jit(solution)/shard_map/while/body/eval_jaxpr/ppermute | solution.py:28
  58.5 5.1 %collective-permute-start = (bf16[1,8,8,128]{3,2,1,0:T(8,128)(2,1)S(1)}, bf16[1,8,8,128]{3,2,1,0:T(8,128)(2,1)S(1)}, u32[]{:S(2)}, u32[]{:S(2)}) collective-permute-start(bf16[1,8,8,128]{3,2,1,0:T(8,128)(2,1)S(1)} %get-tuple-element.462), channel_id=1, source_target_pairs={{1,0},{2,1},{3,2},{4,3},{5,4},{6,5},{7,6},{8,7},{9,8},{10,9},{11,1... | collective-permute-start | bytes 49160 | tf_op jit(solution)/shard_map/while/body/eval_jaxpr/ppermute | solution.py:18
  59.8 4.5 %collective-permute-start.1 = (bf16[1,8,8,128]{3,2,1,0:T(8,128)(2,1)S(1)}, bf16[1,8,8,128]{3,2,1,0:T(8,128)(2,1)S(1)}, u32[]{:S(2)}, u32[]{:S(2)}) collective-permute-start(bf16[1,8,8,128]{3,2,1,0:T(8,128)(2,1)S(1)} %get-tuple-element.463), channel_id=1, source_target_pairs={{0,1},{1,2},{2,3},{3,4},{4,5},{5,6},{6,7},{7,8},{8,9},{9,10},{10,1... | collective-permute-start | bytes 49160 | tf_op jit(solution)/shard_map/while/body/eval_jaxpr/ppermute | solution.py:16
  64.7 1.2 copy-start.4
  66.6 8.1 %collective-permute-start.2 = (bf16[1,8,8,128]{3,2,1,0:T(8,128)(2,1)S(1)}, bf16[1,8,8,128]{3,2,1,0:T(8,128)(2,1)S(1)}, u32[]{:S(2)}, u32[]{:S(2)}) collective-permute-start(bf16[1,8,8,128]{3,2,1,0:T(8,128)(2,1)S(1)} %get-tuple-element.491), channel_id=1, source_target_pairs={{1,0},{2,1},{3,2},{4,3},{5,4},{6,5},{7,6},{8,7},{9,8},{10,9},{11,1... | collective-permute-start | bytes 49160 | tf_op jit(solution)/shard_map/while/body/eval_jaxpr/ppermute | solution.py:18
  67.9 6.9 %collective-permute-start.3 = (bf16[1,8,8,128]{3,2,1,0:T(8,128)(2,1)S(1)}, bf16[1,8,8,128]{3,2,1,0:T(8,128)(2,1)S(1)}, u32[]{:S(2)}, u32[]{:S(2)}) collective-permute-start(bf16[1,8,8,128]{3,2,1,0:T(8,128)(2,1)S(1)} %get-tuple-element.492), channel_id=1, source_target_pairs={{0,1},{1,2},{2,3},{3,4},{4,5},{5,6},{6,7},{7,8},{8,9},{9,10},{10,1... | collective-permute-start | bytes 49160 | tf_op jit(solution)/shard_map/while/body/eval_jaxpr/ppermute | solution.py:16
  76.5 6.2 %collective-permute-start.4 = (bf16[4,8,8,128]{3,2,1,0:T(8,128)(2,1)S(1)}, bf16[4,8,8,128]{3,2,1,0:T(8,128)(2,1)S(1)}, u32[]{:S(2)}, u32[]{:S(2)}) collective-permute-start(bf16[4,8,8,128]{3,2,1,0:T(8,128)(2,1)S(1)} %bitcast.225), channel_id=1, source_target_pairs={{16,0},{17,1},{18,2},{19,3},{20,4},{21,5},{22,6},{23,7},{24,8},{25... | collective-permute-start | bytes 196616 | tf_op jit(solution)/shard_map/while/body/eval_jaxpr/ppermute | solution.py:28
  82.7 1.2 copy-start
  82.7 108.3 %copy-start.3 = (bf16[2,4,8,8,128]{4,3,2,1,0:T(8,128)(2,1)}, bf16[2,4,8,8,128]{4,3,2,1,0:T(8,128)(2,1)S(1)}, u32[]{:S(2)}) copy-start(bf16[2,4,8,8,128]{4,3,2,1,0:T(8,128)(2,1)S(1)} %get-tuple-element.231) | copy-start | bytes 393220
  188.3 9.0 %copy-start.1 = (f32[3456,128]{1,0:T(8,128)S(1)}, f32[3456,128]{1,0:T(8,128)}, u32[]{:S(2)}) copy-start(f32[3456,128]{1,0:T(8,128)} %all-reduce.4.cloned.1.call-done) | copy-start | bytes 5308420
Sparse Core Ops, SparseCore 0:
  84.0 104.2 all-reduce.3
where the time goes:
time: 206 us; the launch traced here: 205 us
  waiting for transfers between devices  121 us (59%)
  starting transfers between devices  38.9 us (19%)
  between operations  14.8 us (7%)
  local copies, waits for them, and re-layouts  11 us (5%)
  matrix products  7.38 us (4%)
  blocking collectives  5.55 us (3%)
  other arithmetic  5.06 us (2%)
    psum x1, waiting for transfers between devices, shards(): summed = lax.psum(partial_value, 'slab')  104 us
    ppermute x6, starting transfers between devices, padded(): lax.ppermute(tail, axis, [(i, (i + 1) % count) for i in range(ends)])  27.3 us
    ppermute x3, waiting for transfers between devices, from_behind(): return lax.ppermute(block, axis, route)  14.5 us
    ppermute x6, starting transfers between devices, padded(): lax.ppermute(head, axis, [((i + 1) % count, i) for i in range(ends)])  7.73 us
    psum x1, blocking collectives, shards(): squares = lax.psum(jnp.sum(summed * summed), 'segment')  5.55 us
    while x159, local copies, waits for them, and re-layouts  4.43 us
  transfers between devices with their start and end apart: 16, of which 7 were waited for; matrix products, arithmetic and copies ran while one was open for 2% of the time, Pallas kernels for 0%

commit v1 on v0

--- a/solution.py
+++ b/solution.py
@@ -110,7 +110,7 @@
     partial_value = final_state[1]
     gradients = final_state[2]
     bound_value = math.sqrt(27.0 * channels * channels * segments)
-    summed = lax.psum(partial_value, "slab")
+    summed = jnp.sum(lax.all_gather(partial_value, "slab"), axis=0)
     squares = lax.psum(jnp.sum(summed * summed), "segment")
     factor = jnp.minimum(1.0, bound_value / (jnp.sqrt(squares) + 1e-06))
     update = summed * factor

time: 206 us -> 262 us (1.27)
  waiting for transfers between devices: 121 us -> 168 us
  other arithmetic: 5.06 us -> 14.2 us
    all_gather x0 -> x1, waiting for transfers between devices: none -> 151 us  [shards(): summed = jnp.sum(lax.all_gather(partial_value, 'slab'), axis=0)]
    psum x1 -> x0, waiting for transfers between devices: 104 us -> none  [shards(): summed = lax.psum(partial_value, 'slab')]
    reduce_sum x0 -> x1, other arithmetic: none -> 10.7 us  [shards(): summed = jnp.sum(lax.all_gather(partial_value, 'slab'), axis=0)]
  transfers between devices with their start and end apart: 16 -> 16, of which waited for: 7 -> 7; matrix products, arithmetic and copies ran while one was open for 2% -> 1% of each run, Pallas kernels for 0% -> 0%
where the time goes in v1:
time: 262 us; the launch traced here: 261 us
  waiting for transfers between devices  168 us (64%)
  starting transfers between devices  38.9 us (15%)
  between operations  14.8 us (6%)
  other arithmetic  14.2 us (5%)
  local copies, waits for them, and re-layouts  11 us (4%)
  matrix products  7.39 us (3%)
  blocking collectives  5.55 us (2%)
    all_gather x1, waiting for transfers between devices, shards(): summed = jnp.sum(lax.all_gather(partial_value, 'slab'), axis=0)  151 us
    ppermute x6, starting transfers between devices, padded(): lax.ppermute(tail, axis, [(i, (i + 1) % count) for i in range(ends)])  27.3 us
    ppermute x3, waiting for transfers between devices, from_behind(): return lax.ppermute(block, axis, route)  14.5 us
    reduce_sum x1, other arithmetic, shards(): summed = jnp.sum(lax.all_gather(partial_value, 'slab'), axis=0)  10.7 us
    ppermute x6, starting transfers between devices, padded(): lax.ppermute(head, axis, [((i + 1) % count, i) for i in range(ends)])  7.73 us
    psum x1, blocking collectives, shards(): squares = lax.psum(jnp.sum(summed * summed), 'segment')  5.55 us
  transfers between devices with their start and end apart: 16, of which 7 were waited for; matrix products, arithmetic and copies ran while one was open for 1% of the time, Pallas kernels for 0%

profile of v1, /device:TPU:0, one launch (start us, length us, event | category | flops | bytes accessed | tf_op | source)
XLA Modules:
  0.0 261.5 jit_solution(8642884717805192174)
XLA Ops:
  7.2 0.0 all-gather.3.cloned.1.call-start
  7.2 2.3 copy.5
  9.5 1.2 rev.3
  10.8 71.9 %while.20 = (s32[]{:T(128)}, bf16[4,8,8,128]{3,2,1,0:T(8,128)(2,1)S(1)}, f32[3456,128]{1,0:T(8,128)S(1)}, bf16[2,4,8,8,128]{4,3,2,1,0:T(8,128)(2,1)S(1)}, pred[]...) while((s32[]{:T(128)}, ...), condition=%wide.region_1.2_spmd.clone, body=%wide.region_0.1_spmd.clone.sunk | while | flops 684656640 | bytes 30519772 | solution.py:109
  10.8 1.3 collective-permute-start
  12.1 3.0 %collective-permute-start.1 = (bf16[1,8,8,128]{3,2,1,0:T(8,128)(2,1)S(1)}, bf16[1,8,8,128]{3,2,1,0:T(8,128)(2,1)S(1)}, u32[]{:S(2)}, u32[]{:S(2)}) collective-permute-start(bf16[1,8,8,128]{3,2,1,0:T(8,128)(2,1)S(1)} %get-tuple-element.463), channel_id=1, source_target_pairs={{0,1},{1,2},{2,3},{3,4},{4,5},{5,6},{6,7},{7,8},{8,9},{9,10},{10,1... | collective-permute-start | bytes 49160 | tf_op jit(solution)/shard_map/while/body/eval_jaxpr/ppermute | solution.py:16
  15.3 0.7 collective-permute-done.1
  16.0 0.1 fusion.54
  16.1 0.1 fusion.55
  16.2 0.2 fusion.56
  17.1 0.5 copy-done.3
  17.6 0.7 fusion.57
  18.3 1.3 collective-permute-start.2
  19.6 5.1 %collective-permute-start.3 = (bf16[1,8,8,128]{3,2,1,0:T(8,128)(2,1)S(1)}, bf16[1,8,8,128]{3,2,1,0:T(8,128)(2,1)S(1)}, u32[]{:S(2)}, u32[]{:S(2)}) collective-permute-start(bf16[1,8,8,128]{3,2,1,0:T(8,128)(2,1)S(1)} %get-tuple-element.492), channel_id=1, source_target_pairs={{0,1},{1,2},{2,3},{3,4},{4,5},{5,6},{6,7},{7,8},{8,9},{9,10},{10,1... | collective-permute-start | bytes 49160 | tf_op jit(solution)/shard_map/while/body/eval_jaxpr/ppermute | solution.py:16
  24.7 1.2 convolution_add_fusion.3
  25.9 0.1 select_maximum_fusion.3
  26.0 0.1 fusion.58
  26.1 0.2 fusion.59
  26.7 0.1 fusion.60
  27.1 0.6 fusion.61
  27.7 1.3 collective-permute-start.4
  29.1 4.8 %collective-permute-done.4 = bf16[4,8,8,128]{3,2,1,0:T(8,128)(2,1)S(1)} collective-permute-done((bf16[4,8,8,128]{3,2,1,0:T(8,128)(2,1)S(1)}, bf16[4,8,8,128]{3,2,1,0:T(8,128)(2,1)S(1)}, u32[]{:S(2)}, u32[]{:S(2)}) %collective-permute-start.4) | collective-permute-done | bytes 65568 | tf_op jit(solution)/shard_map/while/body/eval_jaxpr/ppermute | solution.py:28
  33.9 1.3 collective-permute-start
  35.2 3.7 %collective-permute-start.1 = (bf16[1,8,8,128]{3,2,1,0:T(8,128)(2,1)S(1)}, bf16[1,8,8,128]{3,2,1,0:T(8,128)(2,1)S(1)}, u32[]{:S(2)}, u32[]{:S(2)}) collective-permute-start(bf16[1,8,8,128]{3,2,1,0:T(8,128)(2,1)S(1)} %get-tuple-element.463), channel_id=1, source_target_pairs={{0,1},{1,2},{2,3},{3,4},{4,5},{5,6},{6,7},{7,8},{8,9},{9,10},{10,1... | collective-permute-start | bytes 49160 | tf_op jit(solution)/shard_map/while/body/eval_jaxpr/ppermute | solution.py:16
  39.0 0.7 collective-permute-done.1
  39.7 0.1 fusion.54
  39.8 0.1 fusion.55
  39.8 0.2 fusion.56
  40.8 0.5 copy-done.3
  41.3 0.7 fusion.57
  42.0 1.3 collective-permute-start.2
  43.3 6.1 %collective-permute-start.3 = (bf16[1,8,8,128]{3,2,1,0:T(8,128)(2,1)S(1)}, bf16[1,8,8,128]{3,2,1,0:T(8,128)(2,1)S(1)}, u32[]{:S(2)}, u32[]{:S(2)}) collective-permute-start(bf16[1,8,8,128]{3,2,1,0:T(8,128)(2,1)S(1)} %get-tuple-element.492), channel_id=1, source_target_pairs={{0,1},{1,2},{2,3},{3,4},{4,5},{5,6},{6,7},{7,8},{8,9},{9,10},{10,1... | collective-permute-start | bytes 49160 | tf_op jit(solution)/shard_map/while/body/eval_jaxpr/ppermute | solution.py:16
  49.4 1.2 convolution_add_fusion.3
  50.6 0.1 select_maximum_fusion.3
  50.7 0.1 fusion.58
  50.7 0.2 fusion.59
  51.3 0.1 fusion.60
  51.7 0.6 fusion.61
  52.4 1.3 collective-permute-start.4
  53.7 4.8 %collective-permute-done.4 = bf16[4,8,8,128]{3,2,1,0:T(8,128)(2,1)S(1)} collective-permute-done((bf16[4,8,8,128]{3,2,1,0:T(8,128)(2,1)S(1)}, bf16[4,8,8,128]{3,2,1,0:T(8,128)(2,1)S(1)}, u32[]{:S(2)}, u32[]{:S(2)}) %collective-permute-start.4) | collective-permute-done | bytes 65568 | tf_op jit(solution)/shard_map/while/body/eval_jaxpr/ppermute | solution.py:28
  58.5 1.3 collective-permute-start
  59.8 3.7 %collective-permute-start.1 = (bf16[1,8,8,128]{3,2,1,0:T(8,128)(2,1)S(1)}, bf16[1,8,8,128]{3,2,1,0:T(8,128)(2,1)S(1)}, u32[]{:S(2)}, u32[]{:S(2)}) collective-permute-start(bf16[1,8,8,128]{3,2,1,0:T(8,128)(2,1)S(1)} %get-tuple-element.463), channel_id=1, source_target_pairs={{0,1},{1,2},{2,3},{3,4},{4,5},{5,6},{6,7},{7,8},{8,9},{9,10},{10,1... | collective-permute-start | bytes 49160 | tf_op jit(solution)/shard_map/while/body/eval_jaxpr/ppermute | solution.py:16
  63.6 0.7 collective-permute-done.1
  64.3 0.1 fusion.54
  64.4 0.1 fusion.55
  64.5 0.2 fusion.56
  65.4 0.5 copy-done.3
  65.9 0.7 fusion.57
  66.6 1.3 collective-permute-start.2
  67.9 5.7 %collective-permute-start.3 = (bf16[1,8,8,128]{3,2,1,0:T(8,128)(2,1)S(1)}, bf16[1,8,8,128]{3,2,1,0:T(8,128)(2,1)S(1)}, u32[]{:S(2)}, u32[]{:S(2)}) collective-permute-start(bf16[1,8,8,128]{3,2,1,0:T(8,128)(2,1)S(1)} %get-tuple-element.492), channel_id=1, source_target_pairs={{0,1},{1,2},{2,3},{3,4},{4,5},{5,6},{6,7},{7,8},{8,9},{9,10},{10,1... | collective-permute-start | bytes 49160 | tf_op jit(solution)/shard_map/while/body/eval_jaxpr/ppermute | solution.py:16
  73.6 1.2 convolution_add_fusion.3
  74.8 0.1 select_maximum_fusion.3
  74.9 0.1 fusion.58
  74.9 0.2 fusion.59
  75.5 0.1 fusion.60
  75.9 0.6 fusion.61
  76.6 1.3 collective-permute-start.4
  77.9 4.8 %collective-permute-done.4 = bf16[4,8,8,128]{3,2,1,0:T(8,128)(2,1)S(1)} collective-permute-done((bf16[4,8,8,128]{3,2,1,0:T(8,128)(2,1)S(1)}, bf16[4,8,8,128]{3,2,1,0:T(8,128)(2,1)S(1)}, u32[]{:S(2)}, u32[]{:S(2)}) %collective-permute-start.4) | collective-permute-done | bytes 65568 | tf_op jit(solution)/shard_map/while/body/eval_jaxpr/ppermute | solution.py:28
  82.7 1.2 copy-done
  84.0 151.3 %all-gather.3.cloned.1.call-done = f32[55296,128]{1,0:T(8,128)} async-done(((f32[3456,128]{1,0:T(8,128)}), f32[55296,128]{1,0:T(8,128)}) %all-gather.3.cloned.1.call-update) | async-done | bytes 28311568 | tf_op jit(solution)/shard_map/all_gather | solution.py:113
  235.2 10.7 %reduce_sum.18 = f32[3456,128]{1,0:T(8,128)S(1)} reduce(f32[16,3456,128]{2,1,0:T(8,128)} %bitcast.221, f32[]{:T(128)} %constant.83.clone.1), dimensions={0}, to_apply=%region_2.3 | reduce | flops 6635520 | bytes 30081028 | tf_op jit(solution)/shard_map/reduce_sum | solution.py:113
  246.0 1.1 multiply_reduce_fusion
  247.0 5.5 %psum.7 = f32[]{:T(128)} all-reduce(f32[]{:T(128)} %multiply_reduce_fusion), channel_id=1, replica_groups=mesh['segment'=2,'slab'=16] {'segment'}, use_global_device_ids=true, to_apply=%region_4.5 | all-reduce | flops 1 | bytes 8 | tf_op jit(solution)/shard_map/psum | solution.py:114
  253.3 1.3 multiply_bitcast_fusion
  (206 shorter events, 3.5 us)
Async XLA Ops:
  7.2 228.1 %all-gather.3.cloned.1.call-start = ((), (), s32[]{:S(2)}) async-start(), calls=%async_computation | async-start | bytes 30081024 | tf_op jit(solution)/shard_map/all_gather | solution.py:113
  7.2 3.6 %copy-start.1 = (bf16[1,2,4,8,8,128]{5,4,3,2,1,0:T(8,128)(2,1)S(1)}, bf16[1,2,4,8,8,128]{5,4,3,2,1,0:T(8,128)(2,1)}, u32[]{:S(2)}) copy-start(bf16[1,2,4,8,8,128]{5,4,3,2,1,0:T(8,128)(2,1)} %param.5) | copy-start | bytes 393220
  7.2 3.6 %copy-start.4 = (bf16[2,4,8,8,128]{4,3,2,1,0:T(8,128)(2,1)S(1)}, bf16[2,4,8,8,128]{4,3,2,1,0:T(8,128)(2,1)}, u32[]{:S(2)}) copy-start(bf16[2,4,8,8,128]{4,3,2,1,0:T(8,128)(2,1)} %param.7) | copy-start | bytes 393220
  10.8 4.4 %collective-permute-start = (bf16[1,8,8,128]{3,2,1,0:T(8,128)(2,1)S(1)}, bf16[1,8,8,128]{3,2,1,0:T(8,128)(2,1)S(1)}, u32[]{:S(2)}, u32[]{:S(2)}) collective-permute-start(bf16[1,8,8,128]{3,2,1,0:T(8,128)(2,1)S(1)} %get-tuple-element.462), channel_id=1, source_target_pairs={{1,0},{2,1},{3,2},{4,3},{5,4},{6,5},{7,6},{8,7},{9,8},{10,9},{11,1... | collective-permute-start | bytes 49160 | tf_op jit(solution)/shard_map/while/body/eval_jaxpr/ppermute | solution.py:18
  12.1 3.9 %collective-permute-start.1 = (bf16[1,8,8,128]{3,2,1,0:T(8,128)(2,1)S(1)}, bf16[1,8,8,128]{3,2,1,0:T(8,128)(2,1)S(1)}, u32[]{:S(2)}, u32[]{:S(2)}) collective-permute-start(bf16[1,8,8,128]{3,2,1,0:T(8,128)(2,1)S(1)} %get-tuple-element.463), channel_id=1, source_target_pairs={{0,1},{1,2},{2,3},{3,4},{4,5},{5,6},{6,7},{7,8},{8,9},{9,10},{10,1... | collective-permute-start | bytes 49160 | tf_op jit(solution)/shard_map/while/body/eval_jaxpr/ppermute | solution.py:16
  16.4 1.2 copy-start.3
  18.3 7.6 %collective-permute-start.2 = (bf16[1,8,8,128]{3,2,1,0:T(8,128)(2,1)S(1)}, bf16[1,8,8,128]{3,2,1,0:T(8,128)(2,1)S(1)}, u32[]{:S(2)}, u32[]{:S(2)}) collective-permute-start(bf16[1,8,8,128]{3,2,1,0:T(8,128)(2,1)S(1)} %get-tuple-element.491), channel_id=1, source_target_pairs={{1,0},{2,1},{3,2},{4,3},{5,4},{6,5},{7,6},{8,7},{9,8},{10,9},{11,1... | collective-permute-start | bytes 49160 | tf_op jit(solution)/shard_map/while/body/eval_jaxpr/ppermute | solution.py:18
  19.6 6.3 %collective-permute-start.3 = (bf16[1,8,8,128]{3,2,1,0:T(8,128)(2,1)S(1)}, bf16[1,8,8,128]{3,2,1,0:T(8,128)(2,1)S(1)}, u32[]{:S(2)}, u32[]{:S(2)}) collective-permute-start(bf16[1,8,8,128]{3,2,1,0:T(8,128)(2,1)S(1)} %get-tuple-element.492), channel_id=1, source_target_pairs={{0,1},{1,2},{2,3},{3,4},{4,5},{5,6},{6,7},{7,8},{8,9},{9,10},{10,1... | collective-permute-start | bytes 49160 | tf_op jit(solution)/shard_map/while/body/eval_jaxpr/ppermute | solution.py:16
  27.7 6.2 %collective-permute-start.4 = (bf16[4,8,8,128]{3,2,1,0:T(8,128)(2,1)S(1)}, bf16[4,8,8,128]{3,2,1,0:T(8,128)(2,1)S(1)}, u32[]{:S(2)}, u32[]{:S(2)}) collective-permute-start(bf16[4,8,8,128]{3,2,1,0:T(8,128)(2,1)S(1)} %bitcast.227), channel_id=1, source_target_pairs={{16,0},{17,1},{18,2},{19,3},{20,4},{21,5},{22,6},{23,7},{24,8},{25... | collective-permute-start | bytes 196616 | tf_op jit(solution)/shard_map/while/body/eval_jaxpr/ppermute | solution.py:28
  33.9 5.1 %collective-permute-start = (bf16[1,8,8,128]{3,2,1,0:T(8,128)(2,1)S(1)}, bf16[1,8,8,128]{3,2,1,0:T(8,128)(2,1)S(1)}, u32[]{:S(2)}, u32[]{:S(2)}) collective-permute-start(bf16[1,8,8,128]{3,2,1,0:T(8,128)(2,1)S(1)} %get-tuple-element.462), channel_id=1, source_target_pairs={{1,0},{2,1},{3,2},{4,3},{5,4},{6,5},{7,6},{8,7},{9,8},{10,9},{11,1... | collective-permute-start | bytes 49160 | tf_op jit(solution)/shard_map/while/body/eval_jaxpr/ppermute | solution.py:18
  35.2 4.5 %collective-permute-start.1 = (bf16[1,8,8,128]{3,2,1,0:T(8,128)(2,1)S(1)}, bf16[1,8,8,128]{3,2,1,0:T(8,128)(2,1)S(1)}, u32[]{:S(2)}, u32[]{:S(2)}) collective-permute-start(bf16[1,8,8,128]{3,2,1,0:T(8,128)(2,1)S(1)} %get-tuple-element.463), channel_id=1, source_target_pairs={{0,1},{1,2},{2,3},{3,4},{4,5},{5,6},{6,7},{7,8},{8,9},{9,10},{10,1... | collective-permute-start | bytes 49160 | tf_op jit(solution)/shard_map/while/body/eval_jaxpr/ppermute | solution.py:16
  40.1 1.2 copy-start.3
  42.0 8.6 %collective-permute-start.2 = (bf16[1,8,8,128]{3,2,1,0:T(8,128)(2,1)S(1)}, bf16[1,8,8,128]{3,2,1,0:T(8,128)(2,1)S(1)}, u32[]{:S(2)}, u32[]{:S(2)}) collective-permute-start(bf16[1,8,8,128]{3,2,1,0:T(8,128)(2,1)S(1)} %get-tuple-element.491), channel_id=1, source_target_pairs={{1,0},{2,1},{3,2},{4,3},{5,4},{6,5},{7,6},{8,7},{9,8},{10,9},{11,1... | collective-permute-start | bytes 49160 | tf_op jit(solution)/shard_map/while/body/eval_jaxpr/ppermute | solution.py:18
  43.3 7.3 %collective-permute-start.3 = (bf16[1,8,8,128]{3,2,1,0:T(8,128)(2,1)S(1)}, bf16[1,8,8,128]{3,2,1,0:T(8,128)(2,1)S(1)}, u32[]{:S(2)}, u32[]{:S(2)}) collective-permute-start(bf16[1,8,8,128]{3,2,1,0:T(8,128)(2,1)S(1)} %get-tuple-element.492), channel_id=1, source_target_pairs={{0,1},{1,2},{2,3},{3,4},{4,5},{5,6},{6,7},{7,8},{8,9},{9,10},{10,1... | collective-permute-start | bytes 49160 | tf_op jit(solution)/shard_map/while/body/eval_jaxpr/ppermute | solution.py:16
  52.4 6.2 %collective-permute-start.4 = (bf16[4,8,8,128]{3,2,1,0:T(8,128)(2,1)S(1)}, bf16[4,8,8,128]{3,2,1,0:T(8,128)(2,1)S(1)}, u32[]{:S(2)}, u32[]{:S(2)}) collective-permute-start(bf16[4,8,8,128]{3,2,1,0:T(8,128)(2,1)S(1)} %bitcast.227), channel_id=1, source_target_pairs={{16,0},{17,1},{18,2},{19,3},{20,4},{21,5},{22,6},{23,7},{24,8},{25... | collective-permute-start | bytes 196616 | tf_op jit(solution)/shard_map/while/body/eval_jaxpr/ppermute | solution.py:28
  58.5 5.1 %collective-permute-start = (bf16[1,8,8,128]{3,2,1,0:T(8,128)(2,1)S(1)}, bf16[1,8,8,128]{3,2,1,0:T(8,128)(2,1)S(1)}, u32[]{:S(2)}, u32[]{:S(2)}) collective-permute-start(bf16[1,8,8,128]{3,2,1,0:T(8,128)(2,1)S(1)} %get-tuple-element.462), channel_id=1, source_target_pairs={{1,0},{2,1},{3,2},{4,3},{5,4},{6,5},{7,6},{8,7},{9,8},{10,9},{11,1... | collective-permute-start | bytes 49160 | tf_op jit(solution)/shard_map/while/body/eval_jaxpr/ppermute | solution.py:18
  59.8 4.5 %collective-permute-start.1 = (bf16[1,8,8,128]{3,2,1,0:T(8,128)(2,1)S(1)}, bf16[1,8,8,128]{3,2,1,0:T(8,128)(2,1)S(1)}, u32[]{:S(2)}, u32[]{:S(2)}) collective-permute-start(bf16[1,8,8,128]{3,2,1,0:T(8,128)(2,1)S(1)} %get-tuple-element.463), channel_id=1, source_target_pairs={{0,1},{1,2},{2,3},{3,4},{4,5},{5,6},{6,7},{7,8},{8,9},{9,10},{10,1... | collective-permute-start | bytes 49160 | tf_op jit(solution)/shard_map/while/body/eval_jaxpr/ppermute | solution.py:16
  64.8 1.2 copy-start.3
  66.6 8.1 %collective-permute-start.2 = (bf16[1,8,8,128]{3,2,1,0:T(8,128)(2,1)S(1)}, bf16[1,8,8,128]{3,2,1,0:T(8,128)(2,1)S(1)}, u32[]{:S(2)}, u32[]{:S(2)}) collective-permute-start(bf16[1,8,8,128]{3,2,1,0:T(8,128)(2,1)S(1)} %get-tuple-element.491), channel_id=1, source_target_pairs={{1,0},{2,1},{3,2},{4,3},{5,4},{6,5},{7,6},{8,7},{9,8},{10,9},{11,1... | collective-permute-start | bytes 49160 | tf_op jit(solution)/shard_map/while/body/eval_jaxpr/ppermute | solution.py:18
  67.9 6.9 %collective-permute-start.3 = (bf16[1,8,8,128]{3,2,1,0:T(8,128)(2,1)S(1)}, bf16[1,8,8,128]{3,2,1,0:T(8,128)(2,1)S(1)}, u32[]{:S(2)}, u32[]{:S(2)}) collective-permute-start(bf16[1,8,8,128]{3,2,1,0:T(8,128)(2,1)S(1)} %get-tuple-element.492), channel_id=1, source_target_pairs={{0,1},{1,2},{2,3},{3,4},{4,5},{5,6},{6,7},{7,8},{8,9},{9,10},{10,1... | collective-permute-start | bytes 49160 | tf_op jit(solution)/shard_map/while/body/eval_jaxpr/ppermute | solution.py:16
  76.6 6.2 %collective-permute-start.4 = (bf16[4,8,8,128]{3,2,1,0:T(8,128)(2,1)S(1)}, bf16[4,8,8,128]{3,2,1,0:T(8,128)(2,1)S(1)}, u32[]{:S(2)}, u32[]{:S(2)}) collective-permute-start(bf16[4,8,8,128]{3,2,1,0:T(8,128)(2,1)S(1)} %bitcast.227), channel_id=1, source_target_pairs={{16,0},{17,1},{18,2},{19,3},{20,4},{21,5},{22,6},{23,7},{24,8},{25... | collective-permute-start | bytes 196616 | tf_op jit(solution)/shard_map/while/body/eval_jaxpr/ppermute | solution.py:28
  82.7 1.2 copy-start
  82.7 163.2 %copy-start.2 = (bf16[2,4,8,8,128]{4,3,2,1,0:T(8,128)(2,1)}, bf16[2,4,8,8,128]{4,3,2,1,0:T(8,128)(2,1)S(1)}, u32[]{:S(2)}) copy-start(bf16[2,4,8,8,128]{4,3,2,1,0:T(8,128)(2,1)S(1)} %get-tuple-element.231) | copy-start | bytes 393220
Sparse Core Ops, SparseCore 0:
  84.1 151.1 all-gather.2
